TPU v7x, 256 devices: a whole 4x4x8 slice. The times are simulated.
256 devices in a mesh: dp: 8 (over y, x_lo), tensor: 32 (over x_hi, z, core).
Axes of the slice: x: 4 (x_hi: 2, x_lo: 2; x = x_hi * 2 + x_lo), y: 4, z: 8, core: 2. Of those that a mesh axis runs over, the one named last changes fastest.
Arguments:
- hidden: bfloat16 [6144, 20480], P('dp', 'tensor'), may hold values from -6 to 6
- out_grad: bfloat16 [6144, 8192], P('dp', 'tensor'), may hold values from -6 to 6
- w_down: bfloat16 [20480, 8192], P('tensor'), may hold values from -0.0625 to 0.0625
- proj_in: bfloat16 [64, 20480], P(None, 'tensor'), may hold values from -0.0390625 to 0.0390625
- proj_out: bfloat16 [64, 8192], P(None, 'tensor'), may hold values from -0.0625 to 0.0625
- queries: bfloat16 [1024, 4096], P('tensor'), may hold values from -0.005859375 to 0.005859375
- assignment: int32 [24], replicated, may hold values from 0 to 15
Outputs:
- input_grad: bfloat16 [6144, 20480], P('dp', 'tensor')
- scores: float32 [16, 1024], P('dp', 'tensor')
All inputs are finite; a program needn't handle non-finite values.
Results may differ from a plain program's by a relative error of at most 0.001.
Values may be sent and summed in bfloat16 or wider, within the bound.
No kernel may reach another device: no remote copies, remote signals or barrier semaphores. Data moves between devices by JAX's collectives and lax.ppermute only.
A program may use at most 128 MiB of HBM per device.

v0:
```python
import jax
import jax.numpy as jnp
from jax import lax
from jax.sharding import PartitionSpec as P

LEN = 256
EX_DEV = 2


def on_device(hidden, out_grad, w_down, proj_in, proj_out, queries, assignment):
    tok_rows = hidden.shape[0]
    seq_count = tok_rows // LEN
    act_part = jnp.einsum("tf,kf->tk", hidden, proj_in, preferred_element_type=jnp.float32)
    grad_piece = lax.all_gather(out_grad, "tensor", axis=1, tiled=True)
    proj_piece = lax.all_gather(proj_out, "tensor", axis=1, tiled=True)
    first = jnp.einsum("td,fd->tf", grad_piece, w_down, preferred_element_type=jnp.float32)
    second = jnp.einsum("td,kd->tk", grad_piece, proj_piece, preferred_element_type=jnp.float32)
    act_low = lax.psum(act_part, "tensor")
    input_grad = first.astype(jnp.bfloat16)
    width = act_low.shape[1]
    act_seq = act_low.reshape(seq_count, LEN, width)
    grad_seq = second.reshape(seq_count, LEN, width)
    proj_grads = jnp.einsum(
        "slk,slm->skm", act_seq, grad_seq, precision=lax.Precision.HIGHEST
    ).reshape(seq_count, width * width)
    query_wide = queries.astype(jnp.float32)
    all_grads = lax.all_gather(proj_grads, "dp", axis=0, tiled=True)
    first_example = lax.axis_index("dp") * EX_DEV
    example_ids = first_example + jnp.arange(EX_DEV, dtype=jnp.int32)
    one_hot = (example_ids[:, None] == assignment[None, :]).astype(jnp.float32)
    example_grads = jnp.dot(one_hot, all_grads, precision=lax.Precision.HIGHEST)
    scores = jnp.dot(example_grads, query_wide.T, precision=lax.Precision.HIGHEST)
    return (input_grad, scores)


def solution(mesh):
    placed = (
        P("dp", "tensor"),
        P("dp", "tensor"),
        P("tensor", None),
        P(None, "tensor"),
        P(None, "tensor"),
        P("tensor", None),
        P(),
    )
    return jax.shard_map(
        on_device,
        mesh=mesh,
        in_specs=placed,
        out_specs=(P("dp", "tensor"), P("dp", "tensor")),
        check_vma=False,
    )
```

profile of v0, /device:TPU:4, one launch (start us, length us, event | category | flops | bytes accessed | tf_op | source)
XLA Modules:
  0.0 524.6 jit_solution(11781420502975008039)
XLA Ops:
  7.2 0.0 copy-start
  7.2 0.0 copy-start.1
  7.2 0.0 copy-start.2
  7.2 0.0 all-gather.6.cloned.1.call-start
  7.2 0.7 all-gather.6.cloned.1.call-update
  7.9 0.0 all-gather.4.cloned.1.call-start
  8.0 0.7 all-gather.4.cloned.1.call-update
  8.7 0.0 all-reduce.2.cloned.1.call-start
  8.7 0.0 copy-done
  8.7 1.3 fusion.7
  10.0 0.7 copy.22
  10.7 0.0 all-reduce.2.cloned.1.call-update
  10.8 73.6 %all-gather.6.cloned.1.call-done = bf16[64,8192]{1,0:T(8,128)(2,1)} async-done(((bf16[64,256]{1,0:T(8,128)(2,1)}), bf16[64,8192]{1,0:T(8,128)(2,1)}) %all-gather.6.cloned.1.call-update) | async-done | bytes 1048592 | tf_op jit(solution)/shard_map/all_gather | solution.py:15
  84.3 129.2 %all-gather.4.cloned.1.call-done = bf16[768,8192]{1,0:T(8,128)(2,1)} async-done(((bf16[768,256]{1,0:T(8,128)(2,1)}), bf16[768,8192]{1,0:T(8,128)(2,1)}) %all-gather.4.cloned.1.call-update) | async-done | bytes 12582928 | tf_op jit(solution)/shard_map/all_gather | solution.py:14
  213.5 8.7 %fusion.8 = f32[768,64]{0,1:T(8,128)S(1)} fusion(bf16[768,8192]{1,0:T(8,128)(2,1)} %all-gather.4.cloned.1.call-done, bf16[64,8192]{1,0:T(8,128)(2,1)} %all-gather.6.cloned.1.call-done), kind=kOutput, calls=%fused_computation.11 | convolution fusion | flops 805306368 | bytes 13828096 | tf_op jit(solution)/shard_map/td,kd->tk/dot_general | solution.py:17
  222.3 247.4 %all-reduce.2.cloned.1.call-done = f32[3,256,64]{1,2,0:T(8,128)} async-done(((f32[3,256,64]{1,2,0:T(8,128)}), f32[3,256,64]{1,2,0:T(8,128)}) %all-reduce.2.cloned.1.call-update) | async-done | bytes 196624 | tf_op jit(solution)/shard_map/psum | solution.py:18
  469.7 1.2 fusion
  470.9 0.1 reshape.21
  471.0 30.2 %all-gather = f32[8,3,4096]{2,1,0:T(4,128)S(1)} all-gather(f32[1,3,4096]{2,1,0:T(4,128)S(1)} %reshape.21), channel_id=1, replica_groups=mesh['dp'=8,'tensor'=32] {'dp'}, dimensions={0}, use_global_device_ids=true | all-gather | bytes 442368 | tf_op jit(solution)/shard_map/all_gather | solution.py:27
  501.2 0.2 reshape.22
  501.4 0.0 copy-done.1
  501.4 0.3 fusion.3
  501.7 0.9 fusion.9
  502.6 15.5 %convolution_convert_fusion = bf16[768,640]{1,0:T(8,128)(2,1)} fusion(bf16[768,8192]{1,0:T(8,128)(2,1)} %all-gather.4.cloned.1.call-done, bf16[640,8192]{1,0:T(8,128)(2,1)} %param.9), kind=kOutput, calls=%fused_computation | convolution fusion | flops 8053555200 | bytes 24051712 | tf_op jit(solution)/shard_map/td,fd->tf/dot_general | solution.py:16
  (2 shorter events, 0.0 us)
Async XLA Ops:
  7.2 1.6 copy-start
  7.2 494.2 %copy-start.1 = (s32[24]{0:T(128)S(1)}, s32[24]{0:T(128)}, u32[]{:S(2)}) copy-start(s32[24]{0:T(128)} %param.13) | copy-start | bytes 292
  7.2 494.5 %copy-start.2 = (bf16[32,4096]{1,0:T(8,128)(2,1)S(1)}, bf16[32,4096]{1,0:T(8,128)(2,1)}, u32[]{:S(2)}) copy-start(bf16[32,4096]{1,0:T(8,128)(2,1)} %param.12) | copy-start | bytes 786436
  7.2 77.1 %all-gather.6.cloned.1.call-start = ((), (), s32[]{:S(2)}) async-start(), calls=%async_computation.2 | async-start | bytes 1081344 | tf_op jit(solution)/shard_map/all_gather | solution.py:15
  7.9 205.6 %all-gather.4.cloned.1.call-start = ((), (), s32[]{:S(2)}) async-start(), calls=%async_computation | async-start | bytes 12976128 | tf_op jit(solution)/shard_map/all_gather | solution.py:14
  8.7 461.0 %all-reduce.2.cloned.1.call-start = ((), (), s32[]{:S(2)}) async-start(), calls=%async_computation.1 | async-start | bytes 393216 | tf_op jit(solution)/shard_map/psum | solution.py:18
Sparse Core Ops, SparseCore 0:
  10.6 73.7 all-gather.5
  86.9 126.5 all-gather.3
  216.7 252.9 all-reduce.1
where the time goes:
time: 525 us
  waiting for transfers between devices  452 us (86%)
  blocking collectives  30.2 us (6%)
  matrix products  27.9 us (5%)
  between operations  13.8 us (3%)
    psum x1, waiting for transfers between devices, on_device(): act_low = lax.psum(act_part, 'tensor')  247 us
    all_gather x1, waiting for transfers between devices, on_device(): grad_piece = lax.all_gather(out_grad, 'tensor', axis=1, tiled=True)  129 us
    all_gather x1, waiting for transfers between devices, on_device(): proj_piece = lax.all_gather(proj_out, 'tensor', axis=1, tiled=True)  73.6 us
    all_gather x1, blocking collectives, on_device(): all_grads = lax.all_gather(proj_grads, 'dp', axis=0, tiled=True)  30.2 us
    dot_general x1, matrix products, on_device(): jnp.einsum('td,fd->tf', grad_piece, w_down, preferred_element_type=jnp.fl...  15.5 us
  transfers between devices with their start and end apart: 3, of which 3 were waited for; matrix products, arithmetic and copies ran while one was open for 2% of the time, Pallas kernels for 0%

commit v1 on v0

--- a/solution.py
+++ b/solution.py
@@ -15,7 +15,7 @@
     proj_piece = lax.all_gather(proj_out, "tensor", axis=1, tiled=True)
     first = jnp.einsum("td,fd->tf", grad_piece, w_down, preferred_element_type=jnp.float32)
     second = jnp.einsum("td,kd->tk", grad_piece, proj_piece, preferred_element_type=jnp.float32)
-    act_low = lax.psum(act_part, "tensor")
+    act_low = jnp.sum(lax.all_gather(act_part, "tensor"), axis=0)
     input_grad = first.astype(jnp.bfloat16)
     width = act_low.shape[1]
     act_seq = act_low.reshape(seq_count, LEN, width)

time: 525 us -> 373 us (0.71)
  waiting for transfers between devices: 452 us -> 292 us
    psum x1 -> x0, waiting for transfers between devices: 247 us -> none  [on_device(): act_low = lax.psum(act_part, 'tensor')]
    all_gather x0 -> x1, waiting for transfers between devices: none -> 94.5 us  [on_device(): act_low = jnp.sum(lax.all_gather(act_part, 'tensor'), axis=0)]
    all_gather x1, waiting for transfers between devices: 73.6 us -> 66.9 us  [on_device(): proj_piece = lax.all_gather(proj_out, 'tensor', axis=1, tiled=True)]
    unnamed x8 -> x9, local copies, waits for them, and re-layouts: 0.32 us -> 6.12 us
  transfers between devices with their start and end apart: 3 -> 3, of which waited for: 3 -> 3; matrix products, arithmetic and copies ran while one was open for 2% -> 1% of each run, Pallas kernels for 0% -> 0%
where the time goes in v1:
time: 373 us; the launch traced here: 371 us
  waiting for transfers between devices  292 us (78%)
  blocking collectives  30.2 us (8%)
  matrix products  27.7 us (7%)
  between operations  13.8 us (4%)
  local copies, waits for them, and re-layouts  6.12 us (2%)
    all_gather x1, waiting for transfers between devices, on_device(): grad_piece = lax.all_gather(out_grad, 'tensor', axis=1, tiled=True)  129 us
    all_gather x1, waiting for transfers between devices, on_device(): act_low = jnp.sum(lax.all_gather(act_part, 'tensor'), axis=0)  94.5 us
    all_gather x1, waiting for transfers between devices, on_device(): proj_piece = lax.all_gather(proj_out, 'tensor', axis=1, tiled=True)  66.9 us
    all_gather x1, blocking collectives, on_device(): all_grads = lax.all_gather(proj_grads, 'dp', axis=0, tiled=True)  30.2 us
    dot_general x1, matrix products, on_device(): jnp.einsum('td,fd->tf', grad_piece, w_down, preferred_element_type=jnp.fl...  15.5 us
    dot_general x1, matrix products, on_device(): jnp.einsum('td,kd->tk', grad_piece, proj_piece, preferred_element_type=jn...  8.72 us
  transfers between devices with their start and end apart: 3, of which 3 were waited for; matrix products, arithmetic and copies ran while one was open for 1% of the time, Pallas kernels for 0%

profile of v1, /device:TPU:4, one launch (start us, length us, event | category | flops | bytes accessed | tf_op | source)
XLA Modules:
  0.0 370.7 jit_solution(8555874523316764895)
XLA Ops:
  7.2 0.0 copy-start
  7.2 0.0 all-gather.10.cloned.1.call-start
  7.2 1.1 copy-done
  8.4 2.0 fusion.9
  10.4 0.0 all-gather.10.cloned.1.call-update
  10.4 0.0 all-gather.8.cloned.1.call-start
  10.4 0.7 all-gather.8.cloned.1.call-update
  11.1 0.0 all-gather.6.cloned.1.call-start
  11.2 0.7 all-gather.6.cloned.1.call-update
  11.9 94.5 %all-gather.10.cloned.1.call-done = f32[24576,64]{0,1:T(8,128)} async-done(((f32[768,64]{0,1:T(8,128)}), f32[24576,64]{0,1:T(8,128)}) %all-gather.10.cloned.1.call-update) | async-done | bytes 6291472 | tf_op jit(solution)/shard_map/all_gather | solution.py:18
  106.3 4.7 %copy.16 = f32[8,8,32,768]{3,2,1,0:T(8,128)S(1)} copy(f32[8,8,32,768]{3,1,2,0:T(8,128)} %bitcast.22) | data formatting | bytes 12582912
  111.0 0.0 copy-start.1
  111.0 0.0 copy-start.2
  111.0 0.9 bitcast_reduce_fusion
  111.9 66.9 %all-gather.8.cloned.1.call-done = bf16[64,8192]{1,0:T(8,128)(2,1)} async-done(((bf16[64,256]{1,0:T(8,128)(2,1)}), bf16[64,8192]{1,0:T(8,128)(2,1)}) %all-gather.8.cloned.1.call-update) | async-done | bytes 1048592 | tf_op jit(solution)/shard_map/all_gather | solution.py:15
  178.8 129.2 %all-gather.6.cloned.1.call-done = bf16[768,8192]{1,0:T(8,128)(2,1)} async-done(((bf16[768,256]{1,0:T(8,128)(2,1)}), bf16[768,8192]{1,0:T(8,128)(2,1)}) %all-gather.6.cloned.1.call-update) | async-done | bytes 12582928 | tf_op jit(solution)/shard_map/all_gather | solution.py:14
  308.0 8.7 %fusion.10 = f32[768,64]{0,1:T(8,128)S(1)} fusion(bf16[768,8192]{1,0:T(8,128)(2,1)} %all-gather.6.cloned.1.call-done, bf16[64,8192]{1,0:T(8,128)(2,1)} %all-gather.8.cloned.1.call-done), kind=kOutput, calls=%fused_computation.13 | convolution fusion | flops 805306368 | bytes 13828096 | tf_op jit(solution)/shard_map/td,kd->tk/dot_general | solution.py:17
  316.7 0.3 fusion
  317.1 0.1 reshape.22
  317.2 30.2 %all-gather.1 = f32[8,3,4096]{2,1,0:T(4,128)S(1)} all-gather(f32[1,3,4096]{2,1,0:T(4,128)S(1)} %reshape.22), channel_id=1, replica_groups=mesh['dp'=8,'tensor'=32] {'dp'}, dimensions={0}, use_global_device_ids=true | all-gather | bytes 442368 | tf_op jit(solution)/shard_map/all_gather | solution.py:27
  347.3 0.2 reshape.23
  347.6 0.3 fusion.5
  347.8 0.9 fusion.11
  348.7 15.5 %convolution_convert_fusion = bf16[768,640]{1,0:T(8,128)(2,1)} fusion(bf16[768,8192]{1,0:T(8,128)(2,1)} %all-gather.6.cloned.1.call-done, bf16[640,8192]{1,0:T(8,128)(2,1)} %param.9), kind=kOutput, calls=%fused_computation.1 | convolution fusion | flops 8053555200 | bytes 24051712 | tf_op jit(solution)/shard_map/td,fd->tf/dot_general | solution.py:16
  (3 shorter events, 0.0 us)
Async XLA Ops:
  7.2 1.2 copy-start
  7.2 99.2 %all-gather.10.cloned.1.call-start = ((), (), s32[]{:S(2)}) async-start(), calls=%async_computation.2 | async-start | bytes 6488064 | tf_op jit(solution)/shard_map/all_gather | solution.py:18
  10.4 168.4 %all-gather.8.cloned.1.call-start = ((), (), s32[]{:S(2)}) async-start(), calls=%async_computation.1 | async-start | bytes 1081344 | tf_op jit(solution)/shard_map/all_gather | solution.py:15
  11.1 296.9 %all-gather.6.cloned.1.call-start = ((), (), s32[]{:S(2)}) async-start(), calls=%async_computation | async-start | bytes 12976128 | tf_op jit(solution)/shard_map/all_gather | solution.py:14
  111.0 236.5 %copy-start.1 = (s32[24]{0:T(128)S(1)}, s32[24]{0:T(128)}, u32[]{:S(2)}) copy-start(s32[24]{0:T(128)} %param.13) | copy-start | bytes 292
  111.0 236.8 %copy-start.2 = (bf16[32,4096]{1,0:T(8,128)(2,1)S(1)}, bf16[32,4096]{1,0:T(8,128)(2,1)}, u32[]{:S(2)}) copy-start(bf16[32,4096]{1,0:T(8,128)(2,1)} %param.12) | copy-start | bytes 786436
Sparse Core Ops, SparseCore 0:
  11.3 95.0 all-gather.9
  108.9 69.8 all-gather.7
  181.4 126.5 all-gather.5

commit v2 on v0

--- a/solution.py
+++ b/solution.py
@@ -11,7 +11,9 @@
     tok_rows = hidden.shape[0]
     seq_count = tok_rows // LEN
     act_part = jnp.einsum("tf,kf->tk", hidden, proj_in, preferred_element_type=jnp.float32)
-    grad_piece = lax.all_gather(out_grad, "tensor", axis=1, tiled=True)
+    grad_piece = jnp.concatenate(
+        lax.all_to_all(jnp.stack([out_grad] * lax.axis_size("tensor")), "tensor", 0, 0), axis=1
+    )
     proj_piece = lax.all_gather(proj_out, "tensor", axis=1, tiled=True)
     first = jnp.einsum("td,fd->tf", grad_piece, w_down, preferred_element_type=jnp.float32)
     second = jnp.einsum("td,kd->tk", grad_piece, proj_piece, preferred_element_type=jnp.float32)

time: 525 us -> 487 us (0.928)
  waiting for transfers between devices: 452 us -> 358 us
  local copies, waits for them, and re-layouts: 1.02 us -> 44.7 us
  starting transfers between devices: 0.11 us -> 11.9 us
    all_to_all x0 -> x1, waiting for transfers between devices: none -> 279 us  [on_device(): lax.all_to_all(jnp.stack([out_grad] * lax.axis_size('tensor')), 'tensor',...]
    psum x1, waiting for transfers between devices: 247 us -> 78 us  [on_device(): act_low = lax.psum(act_part, 'tensor')]
    all_gather x1 -> x0, waiting for transfers between devices: 129 us -> none  [on_device(): grad_piece = lax.all_gather(out_grad, 'tensor', axis=1, tiled=True)]
    all_gather x1, waiting for transfers between devices: 73.6 us -> 0.01 us  [on_device(): proj_piece = lax.all_gather(proj_out, 'tensor', axis=1, tiled=True)]
    dot_general x0 -> x1, local copies, waits for them, and re-layouts: none -> 19.6 us  [on_device(): jnp.einsum('td,kd->tk', grad_piece, proj_piece, preferred_element_type=jn...]
    reshape x0 -> x1, local copies, waits for them, and re-layouts: none -> 17 us  [on_device(): jnp.concatenate(lax.all_to_all(jnp.stack([out_grad] * lax.axis_size('tens...]
    all_to_all x0 -> x1, starting transfers between devices: none -> 11.8 us  [on_device(): lax.all_to_all(jnp.stack([out_grad] * lax.axis_size('tensor')), 'tensor',...]
    another operation x0 -> x1, local copies, waits for them, and re-layouts: none -> 5.9 us  [on_device(): jnp.stack([out_grad] * lax.axis_size('tensor'))]
  transfers between devices with their start and end apart: 3 -> 3, of which waited for: 3 -> 2; matrix products, arithmetic and copies ran while one was open for 2% -> 10% of each run, Pallas kernels for 0% -> 0%
where the time goes in v2:
time: 487 us; the launch traced here: 486 us
  waiting for transfers between devices  358 us (74%)
  local copies, waits for them, and re-layouts  44.7 us (9%)
  blocking collectives  30.2 us (6%)
  matrix products  27.1 us (6%)
  between operations  14.1 us (3%)
  starting transfers between devices  11.9 us (2%)
    all_to_all x1, waiting for transfers between devices, on_device(): lax.all_to_all(jnp.stack([out_grad] * lax.axis_size('tensor')), 'tensor',...  279 us
    psum x1, waiting for transfers between devices, on_device(): act_low = lax.psum(act_part, 'tensor')  78 us
    all_gather x1, blocking collectives, on_device(): all_grads = lax.all_gather(proj_grads, 'dp', axis=0, tiled=True)  30.2 us
    dot_general x1, local copies, waits for them, and re-layouts, on_device(): jnp.einsum('td,kd->tk', grad_piece, proj_piece, preferred_element_type=jn...  19.6 us
    reshape x1, local copies, waits for them, and re-layouts, on_device(): jnp.concatenate(lax.all_to_all(jnp.stack([out_grad] * lax.axis_size('tens...  17 us
    dot_general x1, matrix products, on_device(): jnp.einsum('td,fd->tf', grad_piece, w_down, preferred_element_type=jnp.fl...  15.5 us
    all_to_all x1, starting transfers between devices, on_device(): lax.all_to_all(jnp.stack([out_grad] * lax.axis_size('tensor')), 'tensor',...  11.8 us
  transfers between devices with their start and end apart: 3, of which 2 were waited for; matrix products, arithmetic and copies ran while one was open for 10% of the time, Pallas kernels for 0%

profile of v2, /device:TPU:4, one launch (start us, length us, event | category | flops | bytes accessed | tf_op | source)
XLA Modules:
  0.0 486.0 jit_solution(8541443015016455069)
XLA Ops:
  7.2 0.0 copy-start
  7.2 1.2 copy.13
  8.4 5.9 %stack.2 = bf16[32,768,256]{1,2,0:T(8,128)(2,1)} broadcast(bf16[768,256]{0,1:T(8,128)(2,1)S(1)} %copy.13), dimensions={1,2} | broadcast | bytes 12976128 | tf_op jit(solution)/shard_map/stack | solution.py:15
  14.3 11.8 %all-to-all-start = ((bf16[32,768,256]{1,2,0:T(8,128)(2,1)}), bf16[32,768,256]{1,2,0:T(8,128)(2,1)}, u32[]{:S(2)}, u32[]{:S(2)}) async-start(bf16[32,768,256]{1,2,0:T(8,128)(2,1)} %stack.2), calls=%async_computation | async-start | bytes 25165824 | tf_op jit(solution)/shard_map/all_to_all | solution.py:15
  26.1 0.0 all-gather.3.cloned.1.call-start
  26.2 0.7 all-gather.3.cloned.1.call-update
  26.9 0.0 all-reduce.2.cloned.1.call-start
  26.9 0.4 fusion.6
  27.3 0.7 copy.18
  28.0 0.0 all-reduce.2.cloned.1.call-update
  28.1 279.3 %all-to-all-done = bf16[32,768,256]{1,2,0:T(8,128)(2,1)} async-done(((bf16[32,768,256]{1,2,0:T(8,128)(2,1)}), bf16[32,768,256]{1,2,0:T(8,128)(2,1)}, u32[]{:S(2)}, u32[]{:S(2)}) %all-to-all-start) | async-done | bytes 12582944 | tf_op jit(solution)/shard_map/all_to_all | solution.py:15
  307.4 17.0 %copy.15 = bf16[768,32,256]{2,1,0:T(8,128)(2,1)} copy(bf16[768,32,256]{0,2,1:T(8,128)(2,1)} %bitcast) | data formatting | bytes 25165824 | tf_op jit(solution)/shard_map/reshape | solution.py:14
  324.4 19.6 %dot_general.22 = bf16[3,256,8192]{2,1,0:T(8,128)(2,1)} reshape(bf16[768,32,256]{2,1,0:T(8,128)(2,1)} %copy.15) | data formatting | bytes 25165824 | tf_op jit(solution)/shard_map/td,kd->tk/dot_general | solution.py:19
  343.9 8.7 %fusion = f32[3,256,64]{1,2,0:T(8,128)S(1)} fusion(bf16[3,256,8192]{2,1,0:T(8,128)(2,1)} %dot_general.22, bf16[64,8192]{1,0:T(8,128)(2,1)} %all-gather.3.cloned.1.call-done), kind=kOutput, calls=%fused_computation.1 | convolution fusion | flops 805306368 | bytes 13828096 | tf_op jit(solution)/shard_map/td,kd->tk/dot_general | solution.py:19
  352.7 78.0 %all-reduce.2.cloned.1.call-done = f32[3,256,64]{1,2,0:T(8,128)} async-done(((f32[3,256,64]{1,2,0:T(8,128)}), f32[3,256,64]{1,2,0:T(8,128)}) %all-reduce.2.cloned.1.call-update) | async-done | bytes 196624 | tf_op jit(solution)/shard_map/psum | solution.py:20
  430.7 1.2 fusion.7
  431.9 0.1 reshape.30
  432.0 30.2 %all-gather = f32[8,3,4096]{2,1,0:T(4,128)S(1)} all-gather(f32[1,3,4096]{2,1,0:T(4,128)S(1)} %reshape.30), channel_id=1, replica_groups=mesh['dp'=8,'tensor'=32] {'dp'}, dimensions={0}, use_global_device_ids=true | all-gather | bytes 442368 | tf_op jit(solution)/shard_map/all_gather | solution.py:29
  462.2 0.2 reshape.31
  462.4 0.0 copy-start.2
  462.4 0.0 copy-start.3
  462.4 15.5 %convolution_convert_fusion = bf16[768,640]{1,0:T(8,128)(2,1)} fusion(bf16[768,8192]{0,1:T(8,128)(2,1)} %bitcast.1, bf16[640,8192]{1,0:T(8,128)(2,1)} %param.9), kind=kOutput, calls=%fused_computation | convolution fusion | flops 8053555200 | bytes 24051712 | tf_op jit(solution)/shard_map/td,fd->tf/dot_general | solution.py:18
  478.0 0.3 fusion.2
  478.3 0.9 fusion.8
  (7 shorter events, 0.0 us)
Async XLA Ops:
  7.2 19.7 %copy-start = (bf16[768,640]{1,0:T(8,128)(2,1)S(1)}, bf16[768,640]{1,0:T(8,128)(2,1)}, u32[]{:S(2)}) copy-start(bf16[768,640]{1,0:T(8,128)(2,1)} %param.7) | copy-start | bytes 2949124
  14.3 12.6 %copy-start.1 = (bf16[64,640]{1,0:T(8,128)(2,1)S(1)}, bf16[64,640]{1,0:T(8,128)(2,1)}, u32[]{:S(2)}) copy-start(bf16[64,640]{1,0:T(8,128)(2,1)} %param.10) | copy-start | bytes 245764
  14.3 293.0 %all-to-all-start = ((bf16[32,768,256]{1,2,0:T(8,128)(2,1)}), bf16[32,768,256]{1,2,0:T(8,128)(2,1)}, u32[]{:S(2)}, u32[]{:S(2)}) async-start(bf16[32,768,256]{1,2,0:T(8,128)(2,1)} %stack.2), calls=%async_computation | async-start | bytes 25165824 | tf_op jit(solution)/shard_map/all_to_all | solution.py:15
  26.1 317.8 %all-gather.3.cloned.1.call-start = ((), (), s32[]{:S(2)}) async-start(), calls=%async_computation.2 | async-start | bytes 1081344 | tf_op jit(solution)/shard_map/all_gather | solution.py:17
  26.9 403.8 %all-reduce.2.cloned.1.call-start = ((), (), s32[]{:S(2)}) async-start(), calls=%async_computation.1 | async-start | bytes 393216 | tf_op jit(solution)/shard_map/psum | solution.py:20
  462.4 15.6 %copy-start.2 = (s32[24]{0:T(128)S(1)}, s32[24]{0:T(128)}, u32[]{:S(2)}) copy-start(s32[24]{0:T(128)} %param.13) | copy-start | bytes 292
  462.4 15.8 %copy-start.3 = (bf16[32,4096]{1,0:T(8,128)(2,1)S(1)}, bf16[32,4096]{1,0:T(8,128)(2,1)}, u32[]{:S(2)}) copy-start(bf16[32,4096]{1,0:T(8,128)(2,1)} %param.12) | copy-start | bytes 786436
Sparse Core Ops, SparseCore 0:
  29.5 112.8 all-gather.2
  145.6 285.0 all-reduce.1
